TPU v7x, 128 devices: a whole 4x4x4 slice. The times are simulated.
128 devices in a mesh: band: 16 (over x, z_lo, core), grid: 8 (over y, z_hi).
Axes of the slice: x: 4, y: 4, z: 4 (z_hi: 2, z_lo: 2; z = z_hi * 2 + z_lo), core: 2. Of those that a mesh axis runs over, the one named last changes fastest.
Arguments:
- valence: bfloat16 [32, 2, 160, 160, 160], P('band', None, 'grid'), may hold values from -6 to 6
- conduction: bfloat16 [16, 2, 160, 160, 160], P('band', None, 'grid'), may hold values from -6 to 6
- val_energy: float32 [32], replicated, may hold values from -12 to -1
- cond_energy: float32 [16], replicated, may hold values from 1 to 16
- cond_band: int32 [16], P('band'), may hold values from 0 to 15, each once
- owners: int32 [2], replicated, may hold values from 0 to 15
- gvectors: int32 [3, 4096], replicated, may hold values from 0 to 159, as said below
Outputs:
- chi0: float32 [2, 4096, 4096], P(None, 'grid', 'band')
Inputs may be any that keep to these rules, and one draw needn't show every extreme that they name: `gvectors`: the G-vectors are distinct; each component, read between -80 and 80, lies within -10 to 10. `owners`: each entry is an index along band. `cond_band`: A permutation of the global conduction band numbers.
All inputs are finite; a program needn't handle non-finite values.
Results may differ from a plain program's by a relative error of at most 0.0092.
Values may be sent and summed in bfloat16 or wider, within the bound.
No kernel may reach another device: no remote copies, remote signals or barrier semaphores. Data moves between devices by JAX's collectives and lax.ppermute only.
A program may use at most 192 MiB of HBM per device.

v0:
```python
import math
import jax
import jax.numpy as jnp
from jax import lax
from jax.sharding import PartitionSpec as P

ROUNDS = 2


def from_root(block, axis, owner):
    block = jnp.where(lax.axis_index(axis) == owner, block, jnp.zeros_like(block))
    return lax.psum(block, axis)


def dft_tables(length):
    positions = jnp.arange(length, dtype=jnp.int32)
    phase_index = positions[:, None] * positions[None, :] % length
    angles = phase_index.astype(jnp.float32) * (2.0 * math.pi / length)
    return (jnp.cos(angles).astype(jnp.bfloat16), jnp.sin(angles).astype(jnp.bfloat16))


def wide_table(cos_table, sin_table):
    top_half = jnp.concatenate([cos_table, -sin_table], axis=1)
    low_half = jnp.concatenate([sin_table, cos_table], axis=1)
    return jnp.concatenate([top_half, low_half], axis=0)


def plane_transform(density, wide, cos_table, sin_table):
    length = cos_table.shape[0]
    along_z = jnp.einsum("bxyk,kq->bxyq", density, wide, preferred_element_type=jnp.float32).astype(
        jnp.bfloat16
    )
    cos_part = jnp.einsum("bxyk,yq->bxqk", along_z, cos_table, preferred_element_type=jnp.float32)
    sin_part = jnp.einsum("bxyk,yq->bxqk", along_z, sin_table, preferred_element_type=jnp.float32)
    real_part = cos_part[..., :length] + sin_part[..., length:]
    imag_part = cos_part[..., length:] - sin_part[..., :length]
    return jnp.concatenate([real_part, imag_part], axis=-1).astype(jnp.bfloat16)


def shards(valence, conduction, val_energy, cond_energy, cond_band, owners, gvectors):
    val_dev = valence.shape[0]
    cond_dev = conduction.shape[0]
    x_local = valence.shape[2]
    length = valence.shape[3]
    y_local = length // lax.axis_size("grid")
    grid_pos = lax.axis_index("grid")
    band_pos = lax.axis_index("band")
    cos_table, sin_table = dft_tables(length)
    wide = wide_table(cos_table, sin_table)
    freq_x, freq_y, freq_z = (gvectors[0], gvectors[1], gvectors[2])
    norm_factor = float(length) ** (-1.5)
    pairs_all = ROUNDS * val_dev * cond_dev * lax.axis_size("band")
    cond_numbers = jnp.arange(cond_energy.shape[0], dtype=jnp.int32)
    cond_levels = jnp.sum(
        jnp.where(cond_band[:, None] == cond_numbers[None, :], cond_energy[None, :], 0.0), axis=1
    )
    cond_f = conduction.astype(jnp.float32)[None]
    local_y = freq_y - grid_pos * y_local
    inside = (local_y >= 0) & (local_y < y_local)
    local_y = jnp.clip(local_y, 0, y_local - 1)
    elem_rounds = []
    weight_rounds = []
    for round_no in range(ROUNDS):
        owner_pos = owners[round_no]
        val_bands = from_root(valence, "band", owner_pos)
        val_levels = lax.dynamic_slice_in_dim(val_energy, owner_pos * val_dev, val_dev, 0)
        val_f = val_bands.astype(jnp.float32)[:, None]
        dens_re = val_f[:, :, 0] * cond_f[:, :, 0] + val_f[:, :, 1] * cond_f[:, :, 1]
        dens_im = val_f[:, :, 0] * cond_f[:, :, 1] - val_f[:, :, 1] * cond_f[:, :, 0]
        density = jnp.concatenate([dens_re, dens_im], axis=-1).astype(jnp.bfloat16)
        density = density.reshape(val_dev * cond_dev, x_local, length, 2 * length)
        plane = plane_transform(density, wide, cos_table, sin_table)
        block = lax.all_to_all(plane, "grid", split_axis=2, concat_axis=1, tiled=True)
        cos_part = jnp.einsum("bxyk,xq->bqyk", block, cos_table, preferred_element_type=jnp.float32)
        sin_part = jnp.einsum("bxyk,xq->bqyk", block, sin_table, preferred_element_type=jnp.float32)
        full_re = cos_part[..., :length] + sin_part[..., length:]
        full_im = cos_part[..., length:] - sin_part[..., :length]
        elem_re = jnp.where(inside[None, :], full_re[:, freq_x, local_y, freq_z], 0.0) * norm_factor
        elem_im = jnp.where(inside[None, :], full_im[:, freq_x, local_y, freq_z], 0.0) * norm_factor
        elem_round = jnp.stack([elem_re, elem_im], axis=1)
        elem_rounds.append(elem_round)
        pair_weight = 2.0 / (pairs_all * (val_levels[:, None] - cond_levels[None, :]))
        weight_rounds.append(pair_weight.reshape(val_dev * cond_dev))
    local_elements = jnp.concatenate(elem_rounds, axis=0)
    local_weights = jnp.concatenate(weight_rounds, axis=0)
    summed = lax.psum(local_elements, "grid")
    row_count = summed.shape[2] // lax.axis_size("grid")
    col_count = summed.shape[2] // lax.axis_size("band")
    gathered, all_weights = (
        lax.all_gather(summed, "band", axis=0, tiled=True),
        lax.all_gather(local_weights, "band", axis=0, tiled=True),
    )
    row_block = lax.dynamic_slice_in_dim(gathered, grid_pos * row_count, row_count, 2)
    col_block = lax.dynamic_slice_in_dim(gathered, band_pos * col_count, col_count, 2)
    weighted = row_block * all_weights[:, None, None]
    right_side = jnp.concatenate([col_block[:, 0], col_block[:, 1]], axis=0)
    left_real = jnp.concatenate([weighted[:, 0], weighted[:, 1]], axis=0)
    left_imag = jnp.concatenate([weighted[:, 1], -weighted[:, 0]], axis=0)
    high = lax.Precision.HIGHEST
    chi_re = jnp.einsum("pr,pc->rc", left_real, right_side, precision=high)
    chi_im = jnp.einsum("pr,pc->rc", left_imag, right_side, precision=high)
    return jnp.stack([chi_re, chi_im])


def solution(mesh):
    return jax.shard_map(
        shards,
        mesh=mesh,
        in_specs=(
            P("band", None, "grid", None, None),
            P("band", None, "grid", None, None),
            P(),
            P(),
            P("band"),
            P(),
            P(),
        ),
        out_specs=P(None, "grid", "band"),
        check_vma=False,
    )
```

profile of v0, /device:TPU:1, one launch (start us, length us, event | category | flops | bytes accessed | tf_op | source)
XLA Modules:
  0.0 955.0 jit_solution(14158442999222053255)
XLA Ops:
  9.2 8.4 select_bitcast_fusion.1
  22.5 287.6 %all-reduce.7.cloned.1.call-done = (bf16[2,1,2,20,160,160]{5,4,3,0,2,1:T(8,128)(2,1)}, bf16[2,1,2,20,160,160]{5,4,3,0,2,1:T(8,128)(2,1)}) async-done(((bf16[2,1,2,20,160,160]{5,4,3,0,2,1:T(8,128)(2,1)}, bf16[2,1,2,20,160,160]{5,4,3,0,2,1:T(8,128)(2,1)}), (bf16[2,1,2,20,160,160]{5,4,3,0,2,1:T(8,128)(2,1)}, bf16[2,1,2,20,160,160]{5,4,3,0,2,1:T(8,128)(2,1)})) %all-reduce.7.cloned.1.call-update) | async-done | bytes 8192016 | tf_op jit(solution)/shard_map/psum | solution.py:12
  310.1 9.6 %broadcast_in_dim.74 = f32[2,1,2,20,160,160]{5,4,3,0,2,1:T(8,128)} convert(bf16[2,1,2,20,160,160]{5,4,3,0,2,1:T(8,128)(2,1)} %get-tuple-element.6) | non-fusion elementwise | flops 2048000 | bytes 12288000 | tf_op jit(solution)/shard_map/broadcast_in_dim | solution.py:67
  319.7 6.6 broadcast_in_dim.79
  326.4 16.5 %add_convert_fusion.1 = (bf16[2,20,160,160]{3,2,1,0:T(8,128)(2,1)}, bf16[2,20,160,160]{3,2,1,0:T(8,128)(2,1)}, bf16[2,20,160,160]{3,2,1,0:T(8,128)(2,1)}, bf16[2,20,160,160]{3,2,1,0:T(8,128)(2,1)}) fusion(f32[2,1,2,20,160,160]{5,4,3,0,2,1:T(8,128)} %broadcast_in_dim.74, f32[20,160,160]{2,1,0:T(8,128)} %get-tuple-element.22, ...), kind=kLoop, calls=%fused_computation.24 | loop fusion | flops 16384000 | bytes 28672000 | tf_op jit(solution)/shard_map/convert.9
  342.8 6.2 fusion.32
  357.8 6.1 fusion.1
  363.9 6.9 pad_maximum_fusion.1
  370.8 9.7 %copy.88 = bf16[2,20,160,320]{3,0,1,2:T(2,128)(2,1)} copy(bf16[2,20,160,320]{3,2,1,0:T(8,128)(2,1)} %pad_maximum_fusion.1) | data formatting | bytes 8192000 | tf_op jit(solution)/shard_map/concatenate | solution.py:37
  380.5 7.1 all-to-all-start.1
  401.7 6.0 fusion.3
  407.7 6.9 pad_maximum_fusion
  414.7 9.7 %copy.76 = bf16[2,20,160,320]{3,0,1,2:T(2,128)(2,1)} copy(bf16[2,20,160,320]{3,2,1,0:T(8,128)(2,1)} %pad_maximum_fusion) | data formatting | bytes 8192000 | tf_op jit(solution)/shard_map/concatenate | solution.py:37
  424.4 30.3 %all-to-all-done.1 = bf16[2,20,160,320]{3,0,1,2:T(2,128)(2,1)} async-done(((bf16[2,20,160,320]{3,0,1,2:T(2,128)(2,1)}), bf16[2,20,160,320]{3,0,1,2:T(2,128)(2,1)}, u32[]{:S(2)}, u32[]{:S(2)}) %all-to-all-start.1) | async-done | bytes 4096032 | tf_op jit(solution)/shard_map/all_to_all | solution.py:73
  460.1 7.9 copy.90
  468.0 8.3 fusion.26
  482.1 46.0 %all-to-all-done = bf16[2,20,160,320]{3,0,1,2:T(2,128)(2,1)} async-done(((bf16[2,20,160,320]{3,0,1,2:T(2,128)(2,1)}), bf16[2,20,160,320]{3,0,1,2:T(2,128)(2,1)}, u32[]{:S(2)}, u32[]{:S(2)}) %all-to-all-start) | async-done | bytes 4096032 | tf_op jit(solution)/shard_map/all_to_all | solution.py:73
  528.1 8.0 copy.78
  536.2 8.7 fusion.20
  544.9 5.8 fusion.23
  550.7 9.4 slice_add_fusion
  560.1 10.7 %copy.96 = f32[2,160,20,160]{3,0,2,1:T(2,128)} copy(f32[2,160,20,160]{3,1,2,0:T(8,128)} %get-tuple-element.14) | data formatting | bytes 8192000 | tf_op jit(solution)/shard_map/sub | solution.py:77
  570.7 10.6 %copy.95 = f32[2,160,20,160]{3,0,2,1:T(2,128)} copy(f32[2,160,20,160]{3,1,2,0:T(8,128)} %get-tuple-element.13) | data formatting | bytes 8192000 | tf_op jit(solution)/shard_map/add | solution.py:76
  581.4 51.3 %gather_fusion.3 = f32[4096,2]{0,1:T(2,128)S(1)} fusion(f32[2,160,20,160]{3,0,2,1:T(2,128)} %copy.96, s32[4096]{0:T(1024)S(1)} %bitcast.147), kind=kCustom, calls=%fused_computation.3 | custom fusion | bytes 114688 | tf_op jit(solution)/shard_map/gather | solution.py:79
  632.7 51.4 %gather_fusion.2 = f32[4096,2]{0,1:T(2,128)S(1)} fusion(f32[2,160,20,160]{3,0,2,1:T(2,128)} %copy.95, s32[4096]{0:T(1024)S(1)} %bitcast.148), kind=kCustom, calls=%fused_computation.2 | custom fusion | bytes 114688 | tf_op jit(solution)/shard_map/gather | solution.py:78
  684.1 15.4 %slice_add_fusion.2 = (f32[2,160,20,160]{3,1,2,0:T(8,128)}, f32[2,160,20,160]{3,1,2,0:T(8,128)}) fusion(f32[2,160,20,320]{3,1,2,0:T(8,128)} %fusion.23, f32[2,160,20,320]{3,1,2,0:T(8,128)} %fusion.20), kind=kLoop, calls=%fused_computation.13 | loop fusion | flops 2048000 | bytes 24576000 | tf_op jit(solution)/shard_map/add | solution.py:76
  699.5 10.7 %copy.84 = f32[2,160,20,160]{3,0,2,1:T(2,128)} copy(f32[2,160,20,160]{3,1,2,0:T(8,128)} %get-tuple-element.8) | data formatting | bytes 8192000 | tf_op jit(solution)/shard_map/sub | solution.py:77
  710.2 51.6 %gather_fusion.1 = f32[4096,2]{0,1:T(2,128)S(1)} fusion(f32[2,160,20,160]{3,0,2,1:T(2,128)} %copy.84, s32[4096]{0:T(1024)S(1)} %bitcast.149), kind=kCustom, calls=%fused_computation.1 | custom fusion | bytes 114688 | tf_op jit(solution)/shard_map/gather | solution.py:79
  761.8 10.7 %copy.83 = f32[2,160,20,160]{3,0,2,1:T(2,128)} copy(f32[2,160,20,160]{3,1,2,0:T(8,128)} %get-tuple-element.7) | data formatting | bytes 8192000 | tf_op jit(solution)/shard_map/add | solution.py:76
  772.4 51.3 %gather_fusion = f32[4096,2]{0,1:T(2,128)S(1)} fusion(f32[2,160,20,160]{3,0,2,1:T(2,128)} %copy.83, s32[4096]{0:T(1024)S(1)} %bitcast.150), kind=kCustom, calls=%fused_computation | custom fusion | bytes 114688 | tf_op jit(solution)/shard_map/gather | solution.py:78
  824.6 79.3 %all-reduce.5.cloned.1.call-done = f32[4,2,4096]{2,0,1:T(4,128)} async-done(((f32[4,2,4096]{2,0,1:T(4,128)}), f32[4,2,4096]{2,0,1:T(4,128)}) %all-reduce.5.cloned.1.call-update) | async-done | bytes 131088 | tf_op jit(solution)/shard_map/psum | solution.py:86
  910.4 32.7 %all-reduce = f32[64]{0:T(128)S(1)} all-reduce(f32[64]{0:T(128)S(1)} %maximum_dynamic-update-slice_fusion), channel_id=1, replica_groups=mesh['band'=16,'grid'=8] {'band'}, use_global_device_ids=true, to_apply=%add | all-reduce | flops 64 | bytes 512
  (69 shorter events, 49.7 us)
Async XLA Ops:
  6.5 303.6 %all-reduce.7.cloned.1.call-start = ((), (), s32[]{:S(2)}) async-start(), calls=%async_computation.4 | async-start | bytes 26214400 | tf_op jit(solution)/shard_map/psum | solution.py:12
  17.6 1.9 copy-start.6
  310.1 9.6 %copy-start.4 = (bf16[2,1,2,20,160,160]{5,4,3,0,2,1:T(8,128)(2,1)S(1)}, bf16[2,1,2,20,160,160]{5,4,3,0,2,1:T(8,128)(2,1)}, u32[]{:S(2)}) copy-start(bf16[2,1,2,20,160,160]{5,4,3,0,2,1:T(8,128)(2,1)} %get-tuple-element.5) | copy-start | bytes 12288004
  349.1 2.2 copy-start.3
  380.5 7.1 copy-start.5
  380.5 74.2 %all-to-all-start.1 = ((bf16[2,20,160,320]{3,0,1,2:T(2,128)(2,1)}), bf16[2,20,160,320]{3,0,1,2:T(2,128)(2,1)}, u32[]{:S(2)}, u32[]{:S(2)}) async-start(bf16[2,20,160,320]{3,0,1,2:T(2,128)(2,1)} %copy.88), calls=%async_computation.1 | async-start | bytes 9830400 | tf_op jit(solution)/shard_map/all_to_all | solution.py:73
  392.9 2.3 copy-start.2
  424.4 35.5 %copy-start.7 = (s32[3,4096]{1,0:T(4,128)S(1)}, s32[3,4096]{1,0:T(4,128)}, u32[]{:S(2)}) copy-start(s32[3,4096]{1,0:T(4,128)} %param.13) | copy-start | bytes 147460
  454.7 73.4 %all-to-all-start = ((bf16[2,20,160,320]{3,0,1,2:T(2,128)(2,1)}), bf16[2,20,160,320]{3,0,1,2:T(2,128)(2,1)}, u32[]{:S(2)}, u32[]{:S(2)}) async-start(bf16[2,20,160,320]{3,0,1,2:T(2,128)(2,1)} %copy.76), calls=%async_computation | async-start | bytes 9830400 | tf_op jit(solution)/shard_map/all_to_all | solution.py:73
  459.4 444.6 %all-reduce.5.cloned.1.call-start = ((), (), s32[]{:S(2)}) async-start(), calls=%async_computation.2 | async-start | bytes 262144 | tf_op jit(solution)/shard_map/psum | solution.py:86
  468.0 8.3 copy-start
  536.2 8.7 copy-start.1
  536.2 14.5 %slice-start = ((s8[9830400]{0:T(1024)(128)(4,1)}), s8[4194304]{0:T(1024)(128)(4,1)S(1)}, s32[]{:S(2)}) async-start(s8[9830400]{0:T(1024)(128)(4,1)} %bitcast.151), calls=%async_computation.5 | async-start | bytes 8388608
  536.2 14.5 %slice-start.1 = ((s8[9830400]{0:T(1024)(128)(4,1)}), s8[4194304]{0:T(1024)(128)(4,1)S(1)}, s32[]{:S(2)}) async-start(s8[9830400]{0:T(1024)(128)(4,1)} %bitcast.151), calls=%async_computation.6 | async-start | bytes 8388608
  544.9 5.8 slice-start.2
  772.4 135.2 %copy-start.10 = (u32[128]{0:T(128)S(1)}, u32[128]{0:T(128)}, u32[]{:S(2)}) copy-start(u32[128]{0:T(128)} %constant.132) | copy-start | bytes 1540
  772.4 136.5 %copy-start.9 = (f32[16]{0:T(128)S(1)}, f32[16]{0:T(128)}, u32[]{:S(2)}) copy-start(f32[16]{0:T(128)} %param.10) | copy-start | bytes 196
  772.4 137.1 %copy-start.8 = (f32[32]{0:T(128)S(1)}, f32[32]{0:T(128)}, u32[]{:S(2)}) copy-start(f32[32]{0:T(128)} %param.9) | copy-start | bytes 388
  824.6 118.5 %all-gather.2.cloned.1.call-start = ((), (), s32[]{:S(2)}) async-start(), calls=%async_computation.3 | async-start | bytes 2228224 | tf_op jit(solution)/shard_map/all_gather | solution.py:90
Sparse Core Ops, SparseCore 0:
  17.8 292.2 all-reduce.6
  824.7 79.1 all-reduce.4
  905.8 37.2 all-gather.1
where the time goes:
time: 963 us; the launch traced here: 955 us
  waiting for transfers between devices  443 us (46%)
  local copies, waits for them, and re-layouts  296 us (31%)
  other arithmetic  98.7 us (10%)
  matrix products  54.4 us (6%)
  blocking collectives  32.7 us (3%)
  between operations  17.7 us (2%)
  starting transfers between devices  12.2 us (1%)
    psum x1, waiting for transfers between devices, from_root(): return lax.psum(block, axis)  288 us
    gather x2, local copies, waits for them, and re-layouts, shards(): full_im[:, freq_x, local_y, freq_z]  103 us
    gather x2, local copies, waits for them, and re-layouts, shards(): full_re[:, freq_x, local_y, freq_z]  103 us
    psum x1, waiting for transfers between devices, shards(): summed = lax.psum(local_elements, 'grid')  79.3 us
    all_to_all x2, waiting for transfers between devices, shards(): lax.all_to_all(plane, 'grid', split_axis=2, concat_axis=1, tiled=True)  76.4 us
    unnamed x1, blocking collectives  32.7 us
    another operation x3, other arithmetic  28.6 us
    add x2, other arithmetic, shards(): full_re = cos_part[..., :length] + sin_part[..., length:]  24.8 us
  transfers between devices with their start and end apart: 5, of which 4 were waited for; matrix products, arithmetic and copies ran while one was open for 7% of the time, Pallas kernels for 0%

commit v1 on v0

--- a/solution.py
+++ b/solution.py
@@ -70,7 +70,12 @@
         density = jnp.concatenate([dens_re, dens_im], axis=-1).astype(jnp.bfloat16)
         density = density.reshape(val_dev * cond_dev, x_local, length, 2 * length)
         plane = plane_transform(density, wide, cos_table, sin_table)
-        block = lax.all_to_all(plane, "grid", split_axis=2, concat_axis=1, tiled=True)
+        block = jnp.concatenate(
+            lax.all_to_all(
+                jnp.stack(jnp.split(plane, lax.axis_size("grid"), axis=2)), "grid", 0, 0
+            ),
+            axis=1,
+        )
         cos_part = jnp.einsum("bxyk,xq->bqyk", block, cos_table, preferred_element_type=jnp.float32)
         sin_part = jnp.einsum("bxyk,xq->bqyk", block, sin_table, preferred_element_type=jnp.float32)
         full_re = cos_part[..., :length] + sin_part[..., length:]

time: 963 us -> 959 us (level)
  local copies, waits for them, and re-layouts: 296 us -> 275 us
    concatenate x2 -> x0, local copies, waits for them, and re-layouts: 19.4 us -> none  [plane_transform(): return jnp.concatenate([real_part, imag_part], axis=-1).astype(jnp.bfloat16)]
    another operation x0 -> x2, local copies, waits for them, and re-layouts: none -> 19.3 us  [shards(): jnp.stack(jnp.split(plane, lax.axis_size('grid'), axis=2))]
    unnamed x2 -> x16, other arithmetic: 0.16 us -> 18.4 us
    all_to_all x2 -> x0, local copies, waits for them, and re-layouts: 16 us -> none  [shards(): lax.all_to_all(plane, 'grid', split_axis=2, concat_axis=1, tiled=True)]
    concatenate x2 -> x0, other arithmetic: 13.9 us -> none  [plane_transform(): return jnp.concatenate([real_part, imag_part], axis=-1).astype(jnp.bfloat16)]
    another operation x3 -> x5, other arithmetic: 28.6 us -> 33.5 us
  transfers between devices with their start and end apart: 5 -> 5, of which waited for: 4 -> 5; matrix products, arithmetic and copies ran while one was open for 7% -> 7% of each run, Pallas kernels for 0% -> 0%
where the time goes in v1:
time: 959 us; the launch traced here: 952 us
  waiting for transfers between devices  445 us (46%)
  local copies, waits for them, and re-layouts  275 us (29%)
  other arithmetic  108 us (11%)
  matrix products  61.7 us (6%)
  blocking collectives  32.6 us (3%)
  between operations  17.4 us (2%)
  starting transfers between devices  11.7 us (1%)
    psum x1, waiting for transfers between devices, from_root(): return lax.psum(block, axis)  288 us
    gather x2, local copies, waits for them, and re-layouts, shards(): full_re[:, freq_x, local_y, freq_z]  103 us
    gather x2, local copies, waits for them, and re-layouts, shards(): full_im[:, freq_x, local_y, freq_z]  103 us
    psum x1, waiting for transfers between devices, shards(): summed = lax.psum(local_elements, 'grid')  79 us
    all_to_all x2, waiting for transfers between devices, shards(): lax.all_to_all(jnp.stack(jnp.split(plane, lax.axis_size('grid'), axis=2))...  78.4 us
    unnamed x1, blocking collectives  32.6 us
    another operation x3, other arithmetic  30.7 us
    broadcast_in_dim x3, other arithmetic, shards(): val_f = val_bands.astype(jnp.float32)[:, None]  24.7 us
  transfers between devices with their start and end apart: 5, of which 5 were waited for; matrix products, arithmetic and copies ran while one was open for 7% of the time, Pallas kernels for 0%

profile of v1, /device:TPU:1, one launch (start us, length us, event | category | flops | bytes accessed | tf_op | source)
XLA Modules:
  0.0 952.0 jit_solution(14372033686617017076)
XLA Ops:
  9.1 8.4 select_bitcast_fusion.1
  22.4 287.6 %all-reduce.7.cloned.1.call-done = (bf16[2,1,2,20,160,160]{5,4,3,0,2,1:T(8,128)(2,1)}, bf16[2,1,2,20,160,160]{5,4,3,0,2,1:T(8,128)(2,1)}) async-done(((bf16[2,1,2,20,160,160]{5,4,3,0,2,1:T(8,128)(2,1)}, bf16[2,1,2,20,160,160]{5,4,3,0,2,1:T(8,128)(2,1)}), (bf16[2,1,2,20,160,160]{5,4,3,0,2,1:T(8,128)(2,1)}, bf16[2,1,2,20,160,160]{5,4,3,0,2,1:T(8,128)(2,1)})) %all-reduce.7.cloned.1.call-update) | async-done | bytes 8192016 | tf_op jit(solution)/shard_map/psum | solution.py:12
  310.1 9.6 %broadcast_in_dim.74 = f32[2,1,2,20,160,160]{5,4,3,0,2,1:T(8,128)} convert(bf16[2,1,2,20,160,160]{5,4,3,0,2,1:T(8,128)(2,1)} %get-tuple-element.6) | non-fusion elementwise | flops 2048000 | bytes 12288000 | tf_op jit(solution)/shard_map/broadcast_in_dim | solution.py:67
  319.7 6.7 broadcast_in_dim.79
  326.3 16.6 %add_convert_fusion.1 = (bf16[2,20,160,160]{3,2,1,0:T(8,128)(2,1)}, bf16[2,20,160,160]{3,2,1,0:T(8,128)(2,1)}, bf16[2,20,160,160]{3,2,1,0:T(8,128)(2,1)}, bf16[2,20,160,160]{3,2,1,0:T(8,128)(2,1)}) fusion(f32[2,1,2,20,160,160]{5,4,3,0,2,1:T(8,128)} %broadcast_in_dim.74, f32[20,160,160]{2,1,0:T(8,128)} %get-tuple-element.22, ...), kind=kLoop, calls=%fused_computation.24 | loop fusion | flops 16384000 | bytes 28672000 | tf_op jit(solution)/shard_map/convert.9
  342.9 6.2 fusion.32
  351.3 5.9 convolution_bitcast_fusion.1
  357.1 6.9 fusion.1
  374.6 9.6 %copy.55 = bf16[8,2,20,20,320]{4,1,3,2,0:T(2,128)(2,1)} copy(bf16[8,2,20,20,320]{4,3,2,1,0:T(8,128)(2,1)} %fusion.53) | data formatting | bytes 8192000 | tf_op jit(solution)/shard_map/stack | solution.py:75
  384.2 6.8 all-to-all-start.1
  391.1 5.2 fusion.35
  398.4 5.9 convolution_bitcast_fusion.3
  404.3 7.2 fusion.3
  422.0 9.7 %copy.45 = bf16[8,2,20,20,320]{4,1,3,2,0:T(2,128)(2,1)} copy(bf16[8,2,20,20,320]{4,3,2,1,0:T(8,128)(2,1)} %fusion.55) | data formatting | bytes 8192000 | tf_op jit(solution)/shard_map/stack | solution.py:75
  431.7 26.5 %all-to-all-done.1 = bf16[8,2,20,20,320]{4,1,3,2,0:T(2,128)(2,1)} async-done(((bf16[8,2,20,20,320]{4,1,3,2,0:T(2,128)(2,1)}), bf16[8,2,20,20,320]{4,1,3,2,0:T(2,128)(2,1)}, u32[]{:S(2)}, u32[]{:S(2)}) %all-to-all-start.1) | async-done | bytes 4096032 | tf_op jit(solution)/shard_map/all_to_all | solution.py:74
  463.3 8.2 fusion.26
  471.5 8.2 fusion.29
  479.7 51.9 %all-to-all-done = bf16[8,2,20,20,320]{4,1,3,2,0:T(2,128)(2,1)} async-done(((bf16[8,2,20,20,320]{4,1,3,2,0:T(2,128)(2,1)}), bf16[8,2,20,20,320]{4,1,3,2,0:T(2,128)(2,1)}, u32[]{:S(2)}, u32[]{:S(2)}) %all-to-all-start) | async-done | bytes 4096032 | tf_op jit(solution)/shard_map/all_to_all | solution.py:74
  531.6 8.3 fusion.20
  539.9 8.4 fusion.23
  548.3 9.5 %slice_add_fusion = (f32[2,160,20,160]{3,1,2,0:T(8,128)}, f32[2,160,20,160]{3,1,2,0:T(8,128)}) fusion(f32[2,160,20,320]{3,1,2,0:T(8,128)} %fusion.29, f32[2,160,20,320]{3,1,2,0:T(8,128)S(1)} %bitcast.186), kind=kLoop, calls=%fused_computation.5 | loop fusion | flops 2048000 | bytes 24576000 | tf_op jit(solution)/shard_map/add | solution.py:81
  557.9 10.7 %copy.61 = f32[2,160,20,160]{3,0,2,1:T(2,128)} copy(f32[2,160,20,160]{3,1,2,0:T(8,128)} %get-tuple-element.14) | data formatting | bytes 8192000 | tf_op jit(solution)/shard_map/sub | solution.py:82
  568.6 10.6 %copy.60 = f32[2,160,20,160]{3,0,2,1:T(2,128)} copy(f32[2,160,20,160]{3,1,2,0:T(8,128)} %get-tuple-element.13) | data formatting | bytes 8192000 | tf_op jit(solution)/shard_map/add | solution.py:81
  579.2 51.3 %gather_fusion.3 = f32[4096,2]{0,1:T(2,128)S(1)} fusion(f32[2,160,20,160]{3,0,2,1:T(2,128)} %copy.61, s32[4096]{0:T(1024)S(1)} %bitcast.181), kind=kCustom, calls=%fused_computation.3 | custom fusion | bytes 114688 | tf_op jit(solution)/shard_map/gather | solution.py:84
  630.6 51.6 %gather_fusion.2 = f32[4096,2]{0,1:T(2,128)S(1)} fusion(f32[2,160,20,160]{3,0,2,1:T(2,128)} %copy.60, s32[4096]{0:T(1024)S(1)} %bitcast.182), kind=kCustom, calls=%fused_computation.2 | custom fusion | bytes 114688 | tf_op jit(solution)/shard_map/gather | solution.py:83
  682.1 15.0 %slice_add_fusion.2 = (f32[2,160,20,160]{3,1,2,0:T(8,128)}, f32[2,160,20,160]{3,1,2,0:T(8,128)}) fusion(f32[2,160,20,320]{3,1,2,0:T(8,128)} %fusion.23, f32[2,160,20,320]{3,1,2,0:T(8,128)} %fusion.20), kind=kLoop, calls=%fused_computation.13 | loop fusion | flops 2048000 | bytes 24576000 | tf_op jit(solution)/shard_map/add | solution.py:81
  697.1 10.6 %copy.51 = f32[2,160,20,160]{3,0,2,1:T(2,128)} copy(f32[2,160,20,160]{3,1,2,0:T(8,128)} %get-tuple-element.8) | data formatting | bytes 8192000 | tf_op jit(solution)/shard_map/sub | solution.py:82
  707.7 51.5 %gather_fusion.1 = f32[4096,2]{0,1:T(2,128)S(1)} fusion(f32[2,160,20,160]{3,0,2,1:T(2,128)} %copy.51, s32[4096]{0:T(1024)S(1)} %bitcast.183), kind=kCustom, calls=%fused_computation.1 | custom fusion | bytes 114688 | tf_op jit(solution)/shard_map/gather | solution.py:84
  759.3 10.6 %copy.50 = f32[2,160,20,160]{3,0,2,1:T(2,128)} copy(f32[2,160,20,160]{3,1,2,0:T(8,128)} %get-tuple-element.7) | data formatting | bytes 8192000 | tf_op jit(solution)/shard_map/add | solution.py:81
  769.9 51.4 %gather_fusion = f32[4096,2]{0,1:T(2,128)S(1)} fusion(f32[2,160,20,160]{3,0,2,1:T(2,128)} %copy.50, s32[4096]{0:T(1024)S(1)} %bitcast.184), kind=kCustom, calls=%fused_computation | custom fusion | bytes 114688 | tf_op jit(solution)/shard_map/gather | solution.py:83
  822.2 79.0 %all-reduce.5.cloned.1.call-done = f32[4,2,4096]{2,0,1:T(4,128)} async-done(((f32[4,2,4096]{2,0,1:T(4,128)}), f32[4,2,4096]{2,0,1:T(4,128)}) %all-reduce.5.cloned.1.call-update) | async-done | bytes 131088 | tf_op jit(solution)/shard_map/psum | solution.py:91
  907.6 32.6 %all-reduce = f32[64]{0:T(128)S(1)} all-reduce(f32[64]{0:T(128)S(1)} %maximum_dynamic-update-slice_fusion), channel_id=1, replica_groups=mesh['band'=16,'grid'=8] {'band'}, use_global_device_ids=true, to_apply=%add | all-reduce | flops 64 | bytes 512
  (73 shorter events, 46.1 us)
Async XLA Ops:
  6.5 303.5 %all-reduce.7.cloned.1.call-start = ((), (), s32[]{:S(2)}) async-start(), calls=%async_computation.4 | async-start | bytes 26214400 | tf_op jit(solution)/shard_map/psum | solution.py:12
  17.6 1.9 copy-start.2
  310.1 9.6 %copy-start = (bf16[2,1,2,20,160,160]{5,4,3,0,2,1:T(8,128)(2,1)S(1)}, bf16[2,1,2,20,160,160]{5,4,3,0,2,1:T(8,128)(2,1)}, u32[]{:S(2)}) copy-start(bf16[2,1,2,20,160,160]{5,4,3,0,2,1:T(8,128)(2,1)} %get-tuple-element.5) | copy-start | bytes 12288004
  384.2 6.8 copy-start.1
  384.2 73.9 %all-to-all-start.1 = ((bf16[8,2,20,20,320]{4,1,3,2,0:T(2,128)(2,1)}), bf16[8,2,20,20,320]{4,1,3,2,0:T(2,128)(2,1)}, u32[]{:S(2)}, u32[]{:S(2)}) async-start(bf16[8,2,20,20,320]{4,1,3,2,0:T(2,128)(2,1)} %copy.55), calls=%async_computation.1 | async-start | bytes 9830400 | tf_op jit(solution)/shard_map/all_to_all | solution.py:74
  431.7 31.3 %copy-start.3 = (s32[3,4096]{1,0:T(4,128)S(1)}, s32[3,4096]{1,0:T(4,128)}, u32[]{:S(2)}) copy-start(s32[3,4096]{1,0:T(4,128)} %param.13) | copy-start | bytes 147460
  458.2 73.4 %all-to-all-start = ((bf16[8,2,20,20,320]{4,1,3,2,0:T(2,128)(2,1)}), bf16[8,2,20,20,320]{4,1,3,2,0:T(2,128)(2,1)}, u32[]{:S(2)}, u32[]{:S(2)}) async-start(bf16[8,2,20,20,320]{4,1,3,2,0:T(2,128)(2,1)} %copy.45), calls=%async_computation | async-start | bytes 9830400 | tf_op jit(solution)/shard_map/all_to_all | solution.py:74
  462.8 438.4 %all-reduce.5.cloned.1.call-start = ((), (), s32[]{:S(2)}) async-start(), calls=%async_computation.2 | async-start | bytes 262144 | tf_op jit(solution)/shard_map/psum | solution.py:91
  531.6 16.7 %slice-start = ((s8[9830400]{0:T(1024)(128)(4,1)}), s8[4194304]{0:T(1024)(128)(4,1)S(1)}, s32[]{:S(2)}) async-start(s8[9830400]{0:T(1024)(128)(4,1)} %bitcast.185), calls=%async_computation.5 | async-start | bytes 8388608
  531.6 16.7 %slice-start.1 = ((s8[9830400]{0:T(1024)(128)(4,1)}), s8[4194304]{0:T(1024)(128)(4,1)S(1)}, s32[]{:S(2)}) async-start(s8[9830400]{0:T(1024)(128)(4,1)} %bitcast.185), calls=%async_computation.6 | async-start | bytes 8388608
  539.9 8.4 slice-start.2
  769.9 134.9 %copy-start.6 = (u32[128]{0:T(128)S(1)}, u32[128]{0:T(128)}, u32[]{:S(2)}) copy-start(u32[128]{0:T(128)} %constant.132) | copy-start | bytes 1540
  769.9 136.2 %copy-start.5 = (f32[16]{0:T(128)S(1)}, f32[16]{0:T(128)}, u32[]{:S(2)}) copy-start(f32[16]{0:T(128)} %param.10) | copy-start | bytes 196
  769.9 136.8 %copy-start.4 = (f32[32]{0:T(128)S(1)}, f32[32]{0:T(128)}, u32[]{:S(2)}) copy-start(f32[32]{0:T(128)} %param.9) | copy-start | bytes 388
  822.1 118.2 %all-gather.2.cloned.1.call-start = ((), (), s32[]{:S(2)}) async-start(), calls=%async_computation.3 | async-start | bytes 2228224 | tf_op jit(solution)/shard_map/all_gather | solution.py:95
Sparse Core Ops, SparseCore 0:
  17.7 292.2 all-reduce.6
  822.2 78.9 all-reduce.4
  903.0 37.2 all-gather.1
